TPU v7x, 256 devices: a whole 4x4x8 slice. The times are simulated.
256 devices in a mesh: dp: 32 (over x, z_lo, core), expert: 8 (over y, z_hi).
Axes of the slice: x: 4, y: 4, z: 8 (z_hi: 2, z_lo: 4; z = z_hi * 4 + z_lo), core: 2. Of those that a mesh axis runs over, the one named last changes fastest.
Arguments:
- grad_out: bfloat16 [131072, 3072], P(('dp', 'expert')), may hold values from -0.19921875 to 0.19921875
- expert_ids: int32 [131072, 2], P(('dp', 'expert')), may hold values from 0 to 7, all different within a row; in each aligned block of 512 rows (0 to 511, 512 to 1023, ...) at most 192 rows name the same one
- gate_probs: float32 [131072, 2], P(('dp', 'expert')), may hold values from 0.1 to 1
- saved_gate: bfloat16 [49152, 8, 1024], P('dp', 'expert'), may hold values from -6 to 6
- saved_up: bfloat16 [49152, 8, 1024], P('dp', 'expert'), may hold values from -6 to 6
- master: float32 [8, 1024, 3072], P('expert', 'dp')
- moment_one: float32 [8, 1024, 3072], P('expert', 'dp'), may hold values from -2 to 2
- moment_two: float32 [8, 1024, 3072], P('expert', 'dp'), may hold values from 0.05 to 1
Outputs:
- new_master: float32 [8, 1024, 3072], P('expert', 'dp')
- new_moment_one: float32 [8, 1024, 3072], P('expert', 'dp')
- new_moment_two: float32 [8, 1024, 3072], P('expert', 'dp')
- new_weights: float32 [8, 1024, 3072], P('expert')
Inputs may be any that keep to these rules, and one draw needn't show every extreme that they name: `expert_ids`: in each aligned block of 512 rows (the tokens of one device) no expert is named by more than 192 rows, a bound that some block reaches.
All inputs are finite; a program needn't handle non-finite values.
Results may differ from a plain program's by a relative error of at most 0.00035.
Values may be sent and summed in bfloat16 or wider, within the bound.
A program may use at most 128 MiB of HBM per device.

v0:
```python
import jax
import jax.numpy as jnp
from jax import lax
from jax.sharding import PartitionSpec as P


def local(grad_out, expert_ids, gate_probs, saved_gate, saved_up, master, moment_one, moment_two):
    tok_rows = grad_out.shape[0]
    cap_rows = tok_rows * 3 // 8
    hit = expert_ids == 0
    chosen = jnp.any(hit, axis=1)
    weight = jnp.sum(jnp.where(hit, gate_probs, jnp.float32(0.0)), axis=1)
    slot = jnp.cumsum(chosen.astype(jnp.int32)) - 1
    scaled = (weight[:, None] * grad_out.astype(jnp.float32)).astype(jnp.bfloat16)
    places = jnp.arange(cap_rows, dtype=jnp.int32)
    placing = ((slot[None, :] == places[:, None]) & chosen[None, :]).astype(jnp.bfloat16)
    dispatched = jnp.dot(placing, scaled, preferred_element_type=jnp.float32).astype(jnp.bfloat16)
    slot_rows = saved_gate.shape[0]
    width = saved_gate.shape[2]
    gate_part = saved_gate.reshape(slot_rows, width)
    up_part = saved_up.reshape(slot_rows, width)
    hidden = (jax.nn.silu(gate_part.astype(jnp.float32)) * up_part.astype(jnp.float32)).astype(
        jnp.bfloat16
    )
    contract = (((0,), (0,)), ((), ()))
    everyone = lax.all_gather(dispatched, "expert", axis=0, tiled=True)
    total = lax.dot_general(hidden, everyone, contract, preferred_element_type=jnp.float32)
    grad_slice = lax.psum_scatter(total, "dp", scatter_dimension=0, tiled=True)
    grad = grad_slice.reshape(master.shape)
    new_one = 0.9 * moment_one + 0.1 * grad
    new_two = 0.95 * moment_two + 0.05 * grad * grad
    step = new_one / (1.0 - 0.9**20) / (jnp.sqrt(new_two / (1.0 - 0.95**20)) + 1e-08)
    wrms = jnp.sqrt(jnp.mean(master * master, axis=-1, keepdims=True) + 1e-06)
    srms = jnp.sqrt(jnp.mean(step * step, axis=-1, keepdims=True) + 1e-06)
    factor = jnp.minimum(1.0, 0.02 * wrms / (0.01 * srms))
    new_master = master - 0.01 * factor * step
    gathered = lax.all_gather(new_master, "dp", axis=1, tiled=True)
    return (new_master, new_one, new_two, gathered)


def solution(mesh):
    return jax.shard_map(
        local,
        mesh=mesh,
        in_specs=(
            P(("dp", "expert"), None),
            P(("dp", "expert"), None),
            P(("dp", "expert"), None),
            P("dp", "expert", None),
            P("dp", "expert", None),
            P("expert", "dp", None),
            P("expert", "dp", None),
            P("expert", "dp", None),
        ),
        out_specs=(
            P("expert", "dp", None),
            P("expert", "dp", None),
            P("expert", "dp", None),
            P("expert", None, None),
        ),
        check_vma=False,
    )
```

profile of v0, /device:TPU:1, one launch (start us, length us, event | category | flops | bytes accessed | tf_op | source)
XLA Modules:
  0.0 490.4 jit_solution(2230872570642506750)
XLA Ops:
  7.2 0.0 all-gather.3.cloned.1.call-start
  7.2 0.9 fusion.17
  8.1 0.3 reduce-window.9
  8.4 0.1 slice.7
  8.5 0.1 slice_reduce_fusion
  8.6 0.1 add_bitcast_fusion
  8.7 0.7 select_reduce_fusion
  9.4 3.8 convolution_convert_fusion
  13.2 0.0 all-gather.3.cloned.1.call-update
  13.3 0.0 reduce-scatter.2.cloned.1.call-start
  13.3 193.8 %all-gather.3.cloned.1.call-done = bf16[1536,3072]{1,0:T(8,128)(2,1)} async-done(((bf16[192,3072]{1,0:T(8,128)(2,1)}), bf16[1536,3072]{1,0:T(8,128)(2,1)}) %all-gather.3.cloned.1.call-update) | async-done | bytes 9437200 | tf_op jit(solution)/shard_map/all_gather | solution.py:26
  207.1 17.5 %fusion.5 = f32[1024,3072]{1,0:T(8,128)} fusion(bf16[1536,3072]{1,0:T(8,128)(2,1)} %all-gather.3.cloned.1.call-done, bf16[1536,1,1024]{2,0,1:T(8,128)(2,1)S(1)} %copy-done.5, bf16[1536,1,1024]{2,0,1:T(8,128)(2,1)} %param.11), kind=kOutput, calls=%fused_computation.9 | convolution fusion | flops 9676259328 | bytes 28311552 | tf_op jit(solution)/shard_map/dot_general | solution.py:27
  224.6 0.0 reduce-scatter.2.cloned.1.call-update
  224.7 0.0 all-gather.5.cloned.1.call-start
  224.7 0.9 copy-done
  225.6 0.1 multiply_reduce_fusion.1
  225.8 164.9 %reduce-scatter.2.cloned.1.call-done = f32[32,3072]{1,0:T(8,128)} async-done(((f32[1024,3072]{1,0:T(8,128)}), f32[32,3072]{1,0:T(8,128)}) %reduce-scatter.2.cloned.1.call-update) | async-done | bytes 393232 | tf_op jit(solution)/shard_map/reduce_scatter | solution.py:28
  390.7 0.0 copy-done.4
  390.7 1.4 multiply_reduce_fusion
  392.1 0.0 copy-start.2
  392.1 1.0 multiply_subtract_fusion
  393.1 0.0 all-gather.5.cloned.1.call-update
  393.1 79.8 %all-gather.5.cloned.1.call-done = f32[1,1024,3072]{2,1,0:T(8,128)} async-done(((f32[1,32,3072]{2,1,0:T(8,128)}), f32[1,1024,3072]{2,1,0:T(8,128)}) %all-gather.5.cloned.1.call-update) | async-done | bytes 12582928 | tf_op jit(solution)/shard_map/all_gather | solution.py:37
  472.9 11.0 %copy.13 = f32[1,1024,3072]{2,1,0:T(8,128)} copy(f32[1,1024,3072]{2,1,0:T(8,128)} %all-gather.5.cloned.1.call-done) | data formatting | bytes 25165824
  (12 shorter events, 0.1 us)
Async XLA Ops:
  7.2 200.0 %copy-start.5 = (bf16[1536,1,1024]{2,0,1:T(8,128)(2,1)S(1)}, bf16[1536,1,1024]{2,0,1:T(8,128)(2,1)}, u32[]{:S(2)}) copy-start(bf16[1536,1,1024]{2,0,1:T(8,128)(2,1)} %param.12) | copy-start | bytes 9437188
  7.2 200.0 %all-gather.3.cloned.1.call-start = ((), (), s32[]{:S(2)}) async-start(), calls=%async_computation.1 | async-start | bytes 10616832 | tf_op jit(solution)/shard_map/all_gather | solution.py:26
  13.3 377.4 %reduce-scatter.2.cloned.1.call-start = ((), (), s32[]{:S(2)}) async-start(), calls=%async_computation.2 | async-start | bytes 12976128 | tf_op jit(solution)/shard_map/reduce_scatter | solution.py:28
  224.6 1.0 copy-start
  224.6 166.0 %copy-start.3 = (f32[1,32,3072]{2,1,0:T(8,128)S(1)}, f32[1,32,3072]{2,1,0:T(8,128)}, u32[]{:S(2)}) copy-start(f32[1,32,3072]{2,1,0:T(8,128)} %param.14) | copy-start | bytes 1179652
  224.6 166.0 %copy-start.4 = (f32[1,32,3072]{2,1,0:T(8,128)S(1)}, f32[1,32,3072]{2,1,0:T(8,128)}, u32[]{:S(2)}) copy-start(f32[1,32,3072]{2,1,0:T(8,128)} %param.15) | copy-start | bytes 1179652
  224.7 248.2 %all-gather.5.cloned.1.call-start = ((), (), s32[]{:S(2)}) async-start(), calls=%async_computation.3 | async-start | bytes 12976128 | tf_op jit(solution)/shard_map/all_gather | solution.py:37
  392.0 91.9 %copy-start.1 = (f32[1,32,3072]{2,1,0:T(8,128)}, f32[1,32,3072]{2,1,0:T(8,128)S(1)}, u32[]{:S(2)}) copy-start(f32[1,32,3072]{2,1,0:T(8,128)S(1)} %get-tuple-element.12) | copy-start | bytes 1179652
  392.1 91.9 %copy-start.2 = (f32[1,32,3072]{2,1,0:T(8,128)}, f32[1,32,3072]{2,1,0:T(8,128)S(1)}, u32[]{:S(2)}) copy-start(f32[1,32,3072]{2,1,0:T(8,128)S(1)} %get-tuple-element.13) | copy-start | bytes 1179652
Sparse Core Ops, SparseCore 0:
  13.4 193.7 all-gather.2
  224.8 165.8 reduce-scatter.1
  393.2 79.6 all-gather.4
where the time goes:
time: 491 us; the launch traced here: 490 us
  waiting for transfers between devices  439 us (89%)
  matrix products  21.3 us (4%)
  between operations  13.8 us (3%)
  local copies, waits for them, and re-layouts  12.1 us (2%)
    all_gather x1, waiting for transfers between devices, local(): everyone = lax.all_gather(dispatched, 'expert', axis=0, tiled=True)  194 us
    reduce_scatter x1, waiting for transfers between devices, local(): grad_slice = lax.psum_scatter(total, 'dp', scatter_dimension=0, tiled=True)  165 us
    all_gather x1, waiting for transfers between devices, local(): gathered = lax.all_gather(new_master, 'dp', axis=1, tiled=True)  79.8 us
    dot_general x1, matrix products, local(): lax.dot_general(hidden, everyone, contract, preferred_element_type=jnp.fl...  17.5 us
    unnamed x13, local copies, waits for them, and re-layouts  11.9 us
  transfers between devices with their start and end apart: 3, of which 3 were waited for; matrix products, arithmetic and copies ran while one was open for 0% of the time, Pallas kernels for 0%

commit v1 on v0

--- a/solution.py
+++ b/solution.py
@@ -2,6 +2,16 @@
 import jax.numpy as jnp
 from jax import lax
 from jax.sharding import PartitionSpec as P
+
+
+def answer_the_shards(sheet, dim_i):
+    grid = []
+    for _ in range(lax.axis_size("dp")):
+        grid.append(sheet)
+    parts_out = jnp.stack(grid, axis=0)
+    v_now = lax.all_to_all(parts_out, "dp", 0, 0)
+    known = jnp.concatenate(v_now, axis=dim_i)
+    return known
 
 
 def local(grad_out, expert_ids, gate_probs, saved_gate, saved_up, master, moment_one, moment_two):
@@ -34,7 +44,7 @@
     srms = jnp.sqrt(jnp.mean(step * step, axis=-1, keepdims=True) + 1e-06)
     factor = jnp.minimum(1.0, 0.02 * wrms / (0.01 * srms))
     new_master = master - 0.01 * factor * step
-    gathered = lax.all_gather(new_master, "dp", axis=1, tiled=True)
+    gathered = answer_the_shards(new_master, 1)
     return (new_master, new_one, new_two, gathered)
 
 

time: 491 us -> 695 us (1.42)
  blocking collectives: 0 us -> 283 us
  waiting for transfers between devices: 439 us -> 358 us
    all_to_all x0 -> x1, blocking collectives: none -> 283 us  [answer_the_shards(): v_now = lax.all_to_all(parts_out, 'dp', 0, 0)]
    all_gather x1 -> x0, waiting for transfers between devices: 79.8 us -> none  [local(): gathered = lax.all_gather(new_master, 'dp', axis=1, tiled=True)]
  transfers between devices with their start and end apart: 3 -> 2, of which waited for: 3 -> 2; matrix products, arithmetic and copies ran while one was open for 0% -> 0% of each run, Pallas kernels for 0% -> 0%
where the time goes in v1:
time: 695 us
  waiting for transfers between devices  358 us (52%)
  blocking collectives  283 us (41%)
  matrix products  21.3 us (3%)
  between operations  14.1 us (2%)
  local copies, waits for them, and re-layouts  13.7 us (2%)
    all_to_all x1, blocking collectives, answer_the_shards(): v_now = lax.all_to_all(parts_out, 'dp', 0, 0)  283 us
    all_gather x1, waiting for transfers between devices, local(): everyone = lax.all_gather(dispatched, 'expert', axis=0, tiled=True)  194 us
    reduce_scatter x1, waiting for transfers between devices, local(): grad_slice = lax.psum_scatter(total, 'dp', scatter_dimension=0, tiled=True)  165 us
    dot_general x1, matrix products, local(): lax.dot_general(hidden, everyone, contract, preferred_element_type=jnp.fl...  17.5 us
  transfers between devices with their start and end apart: 2, of which 2 were waited for; matrix products, arithmetic and copies ran while one was open for 0% of the time, Pallas kernels for 0%

profile of v1, /device:TPU:1, one launch (start us, length us, event | category | flops | bytes accessed | tf_op | source)
XLA Modules:
  0.0 694.6 jit_solution(12441485159932107662)
XLA Ops:
  7.2 0.0 all-gather.2.cloned.1.call-start
  7.2 0.9 fusion.17
  8.1 0.3 reduce-window.9
  8.4 0.1 slice.7
  8.5 0.1 slice_reduce_fusion
  8.6 0.1 add_bitcast_fusion
  8.7 0.7 select_reduce_fusion
  9.4 3.8 convolution_convert_fusion
  13.2 0.0 all-gather.2.cloned.1.call-update
  13.3 0.0 reduce-scatter.2.cloned.1.call-start
  13.3 193.8 %all-gather.2.cloned.1.call-done = bf16[1536,3072]{1,0:T(8,128)(2,1)} async-done(((bf16[192,3072]{1,0:T(8,128)(2,1)}), bf16[1536,3072]{1,0:T(8,128)(2,1)}) %all-gather.2.cloned.1.call-update) | async-done | bytes 9437200 | tf_op jit(solution)/shard_map/all_gather | solution.py:36
  207.1 17.5 %fusion.5 = f32[1024,3072]{1,0:T(8,128)} fusion(bf16[1536,3072]{1,0:T(8,128)(2,1)} %all-gather.2.cloned.1.call-done, bf16[1536,1,1024]{2,0,1:T(8,128)(2,1)S(1)} %copy-done.6, bf16[1536,1,1024]{2,0,1:T(8,128)(2,1)} %param.11), kind=kOutput, calls=%fused_computation.9 | convolution fusion | flops 9676259328 | bytes 28311552 | tf_op jit(solution)/shard_map/dot_general | solution.py:37
  224.7 0.0 reduce-scatter.2.cloned.1.call-update
  224.7 1.0 copy-done.1
  225.6 0.1 multiply_reduce_fusion.1
  225.8 164.6 %reduce-scatter.2.cloned.1.call-done = f32[32,3072]{1,0:T(8,128)} async-done(((f32[1024,3072]{1,0:T(8,128)}), f32[32,3072]{1,0:T(8,128)}) %reduce-scatter.2.cloned.1.call-update) | async-done | bytes 393232 | tf_op jit(solution)/shard_map/reduce_scatter | solution.py:38
  390.4 0.0 copy-done.5
  390.4 1.4 multiply_reduce_fusion
  391.8 0.0 copy-start.3
  391.8 0.2 multiply_subtract_fusion
  392.0 0.0 copy-start
  392.0 1.6 stack.2
  393.6 283.1 %all_to_all.5 = f32[32,1,32,3072]{3,2,1,0:T(8,128)} all-to-all(f32[32,1,32,3072]{3,2,1,0:T(8,128)S(1)} %stack.2), channel_id=1, replica_groups=mesh['dp'=32,'expert'=8] {'dp'}, dimensions={0} | all-to-all | bytes 25165824 | tf_op jit(solution)/shard_map/all_to_all | solution.py:12
  676.8 11.0 %copy.13 = f32[1,1024,3072]{2,1,0:T(8,128)} copy(f32[1,1024,3072]{2,1,0:T(8,128)} %bitcast.27) | data formatting | bytes 25165824
  (13 shorter events, 0.1 us)
Async XLA Ops:
  7.2 200.0 %copy-start.6 = (bf16[1536,1,1024]{2,0,1:T(8,128)(2,1)S(1)}, bf16[1536,1,1024]{2,0,1:T(8,128)(2,1)}, u32[]{:S(2)}) copy-start(bf16[1536,1,1024]{2,0,1:T(8,128)(2,1)} %param.12) | copy-start | bytes 9437188
  7.2 200.0 %all-gather.2.cloned.1.call-start = ((), (), s32[]{:S(2)}) async-start(), calls=%async_computation.2 | async-start | bytes 10616832 | tf_op jit(solution)/shard_map/all_gather | solution.py:36
  13.3 377.1 %reduce-scatter.2.cloned.1.call-start = ((), (), s32[]{:S(2)}) async-start(), calls=%async_computation.3 | async-start | bytes 12976128 | tf_op jit(solution)/shard_map/reduce_scatter | solution.py:38
  224.6 1.0 copy-start.1
  224.6 165.7 %copy-start.4 = (f32[1,32,3072]{2,1,0:T(8,128)S(1)}, f32[1,32,3072]{2,1,0:T(8,128)}, u32[]{:S(2)}) copy-start(f32[1,32,3072]{2,1,0:T(8,128)} %param.14) | copy-start | bytes 1179652
  224.6 165.7 %copy-start.5 = (f32[1,32,3072]{2,1,0:T(8,128)S(1)}, f32[1,32,3072]{2,1,0:T(8,128)}, u32[]{:S(2)}) copy-start(f32[1,32,3072]{2,1,0:T(8,128)} %param.15) | copy-start | bytes 1179652
  391.7 1.8 copy-start.2
  391.8 1.8 copy-start.3
  392.0 1.6 copy-start
Sparse Core Ops, SparseCore 0:
  13.4 193.7 all-gather.1
  224.8 165.5 reduce-scatter.1
